TPU v7x, 32 devices: a whole 2x2x4 slice. The times are simulated.
32 devices in a mesh: pipe: 4 (over y, core), expert: 4 (over z), dp: 2 (over x).
Axes of the slice: x: 2, y: 2, z: 4, core: 2. Of those that a mesh axis runs over, the one named last changes fastest.
Arguments:
- acts: bfloat16 [256, 3584], P(('pipe', 'expert', 'dp')), may hold values from -6 to 6
- cotangent: bfloat16 [256, 3584], P(('pipe', 'expert', 'dp')), may hold values from -6 to 6
- routes: int32 [256, 1], P(('pipe', 'expert', 'dp')), may hold values from 0 to 1; in each aligned block of 8 rows (0 to 7, 8 to 15, ...) at most 6 rows name the same one
- probs: bfloat16 [256, 1], P(('pipe', 'expert', 'dp')), may hold values from 0.19921875 to 1
- keep: int32 [4, 8], P('pipe', ('expert', 'dp')), may hold values 0 or 1
- w_gate: bfloat16 [4, 4, 3584, 512], P('pipe', 'expert', None, 'dp'), may hold values from -0.09375 to 0.09375
- w_up: bfloat16 [4, 4, 3584, 512], P('pipe', 'expert', None, 'dp'), may hold values from -0.09375 to 0.09375
- w_down: bfloat16 [4, 4, 512, 3584], P('pipe', 'expert', 'dp'), may hold values from -0.1875 to 0.1875
Outputs:
- layer_out: bfloat16 [256, 3584], P(('pipe', 'expert', 'dp'))
- grad_below: bfloat16 [256, 3584], P(('pipe', 'expert', 'dp'))
Inputs may be any that keep to these rules, and one draw needn't show every extreme that they name: `routes`: the 1 expert of a token differ. Among the rows of one device no expert is named more than 6 times, and in every draw some device names some expert exactly 6 times.
All inputs are finite; a program needn't handle non-finite values. No bound on the sum of `keep` on one device may be relied on, other than what follows from the above.
Results may differ from a plain program's by a relative error of at most 0.0075.
Values may be sent and summed in bfloat16 or wider, within the bound.
No kernel may reach another device: no remote copies, remote signals or barrier semaphores. Data moves between devices by JAX's collectives and lax.ppermute only.
A program may use at most 64 MiB of HBM per device.

v0:
```python
import jax
import jax.numpy as jnp
from jax import lax
from jax.sharding import PartitionSpec as P


def from_behind(shard, axis, by):
    count = lax.axis_size(axis)
    pairs = [(i, i + by) for i in range(count) if 0 <= i + by < count]
    return lax.ppermute(shard, axis, pairs)


def expert_pass(input_rows, rows_cot, gate_cols, up_cols, down_rows):
    contract = (((1,), (1,)), ((), ()))
    gate_pre = jnp.dot(input_rows, gate_cols, preferred_element_type=jnp.float32)
    up_pre = jnp.dot(input_rows, up_cols, preferred_element_type=jnp.float32)
    squash = jax.nn.sigmoid(gate_pre)
    hidden = (gate_pre * squash * up_pre).astype(jnp.bfloat16)
    grad_hidden = lax.dot_general(rows_cot, down_rows, contract, preferred_element_type=jnp.float32)
    grad_gate = (grad_hidden * up_pre * squash * (1.0 + gate_pre * (1.0 - squash))).astype(
        jnp.bfloat16
    )
    grad_up = (grad_hidden * gate_pre * squash).astype(jnp.bfloat16)
    part_out = jnp.dot(hidden, down_rows, preferred_element_type=jnp.float32)
    partial_gradient = lax.dot_general(
        grad_gate, gate_cols, contract, preferred_element_type=jnp.float32
    )
    partial_gradient = partial_gradient + lax.dot_general(
        grad_up, up_cols, contract, preferred_element_type=jnp.float32
    )
    return (part_out, partial_gradient)


def shared_rows(input_rows, rows_cot, gate_cols, up_cols, down_rows):
    every_in, every_cot = (
        lax.all_gather(input_rows, "dp", axis=0, tiled=True),
        lax.all_gather(rows_cot, "dp", axis=0, tiled=True),
    )
    part_out, partial_gradient = expert_pass(every_in, every_cot, gate_cols, up_cols, down_rows)
    summed_out, summed_grad = (
        lax.psum_scatter(
            part_out.astype(jnp.bfloat16), "dp", scatter_dimension=0, tiled=True
        ).astype(jnp.float32),
        lax.psum_scatter(
            partial_gradient.astype(jnp.bfloat16), "dp", scatter_dimension=0, tiled=True
        ).astype(jnp.float32),
    )
    return (summed_out.astype(jnp.bfloat16), summed_grad.astype(jnp.bfloat16))


def shards(acts, cotangent, routes, probs, keep, w_gate, w_up, w_down):
    n_expert = lax.axis_size("expert")
    experts = n_expert // 2
    token_count = acts.shape[0]
    width = acts.shape[1]
    top_count = routes.shape[1]
    capacity = 2 * ((token_count * top_count * 5 + 8 * experts - 1) // (8 * experts))
    slot_count = experts * capacity
    pair_count = token_count * top_count
    chosen = routes.reshape(pair_count)
    weights = probs.reshape(pair_count)
    expert_hot = (chosen[:, None] == jnp.arange(experts, dtype=jnp.int32)[None, :]).astype(
        jnp.int32
    )
    ranks = jnp.cumsum(expert_hot, axis=0) - 1
    placed = jnp.sum(expert_hot * ranks, axis=1)
    target = chosen * capacity + placed
    slot_hot = target[:, None] == jnp.arange(slot_count, dtype=jnp.int32)[None, :]
    owner = jnp.arange(pair_count, dtype=jnp.int32) // top_count
    token_hot = (owner[:, None] == jnp.arange(token_count, dtype=jnp.int32)[None, :]).astype(
        jnp.bfloat16
    )
    scatter_mat = jnp.dot(
        slot_hot.astype(jnp.bfloat16).T, token_hot, preferred_element_type=jnp.float32
    ).astype(jnp.bfloat16)
    weighted_hot = jnp.where(slot_hot, weights[:, None], jnp.zeros((), jnp.bfloat16))
    gather_matrix = jnp.dot(token_hot.T, weighted_hot, preferred_element_type=jnp.float32).astype(
        jnp.bfloat16
    )
    packed_in = jnp.dot(scatter_mat, acts, preferred_element_type=jnp.float32).astype(jnp.bfloat16)
    packed_cot = jnp.dot(scatter_mat, cotangent, preferred_element_type=jnp.float32).astype(
        jnp.bfloat16
    )
    gate_cols = w_gate[0, 0]
    up_cols = w_up[0, 0]
    down_rows = w_down[0, 0]
    send_in = jnp.repeat(packed_in.reshape(experts, capacity, width), 2, axis=0).reshape(
        n_expert * capacity, width
    )
    send_cot = jnp.repeat(packed_cot.reshape(experts, capacity, width), 2, axis=0).reshape(
        n_expert * capacity, width
    )
    got_in, got_cot = (
        lax.all_to_all(send_in, "expert", split_axis=0, concat_axis=0, tiled=True),
        lax.all_to_all(send_cot, "expert", split_axis=0, concat_axis=0, tiled=True),
    )
    half_out, half_grad = shared_rows(got_in, got_cot, gate_cols, up_cols, down_rows)
    back_out, back_grad = (
        lax.all_to_all(half_out, "expert", split_axis=0, concat_axis=0, tiled=True),
        lax.all_to_all(half_grad, "expert", split_axis=0, concat_axis=0, tiled=True),
    )
    expert_out = jnp.sum(back_out.reshape(experts, 2, capacity, width).astype(jnp.float32), axis=1)
    expert_out = expert_out.astype(jnp.bfloat16).reshape(slot_count, width)
    expert_grad = jnp.sum(
        back_grad.reshape(experts, 2, capacity, width).astype(jnp.float32), axis=1
    )
    expert_grad = expert_grad.astype(jnp.bfloat16).reshape(slot_count, width)
    mixed_out = jnp.dot(gather_matrix, expert_out, preferred_element_type=jnp.float32)
    mixed_grad = jnp.dot(gather_matrix, expert_grad, preferred_element_type=jnp.float32)
    keep_scale = keep[0, 0].astype(jnp.float32)
    layer_out = (acts.astype(jnp.float32) + keep_scale * mixed_out).astype(jnp.bfloat16)
    section_grad = (cotangent.astype(jnp.float32) + keep_scale * mixed_grad).astype(jnp.bfloat16)
    grad_below = from_behind(section_grad, "pipe", -1)
    return (layer_out, grad_below)


def solution(mesh):
    return jax.shard_map(
        shards,
        mesh=mesh,
        in_specs=(
            P(("pipe", "expert", "dp"), None),
            P(("pipe", "expert", "dp"), None),
            P(("pipe", "expert", "dp"), None),
            P(("pipe", "expert", "dp"), None),
            P("pipe", ("expert", "dp")),
            P("pipe", "expert", None, "dp"),
            P("pipe", "expert", None, "dp"),
            P("pipe", "expert", "dp", None),
        ),
        out_specs=(P(("pipe", "expert", "dp"), None), P(("pipe", "expert", "dp"), None)),
        check_vma=False,
    )
```

profile of v0, /device:TPU:0, one launch (start us, length us, event | category | flops | bytes accessed | tf_op | source)
XLA Modules:
  0.0 100.5 jit_solution(3909824233218656353)
XLA Ops:
  7.2 0.8 fusion.24
  8.0 0.2 reduce_window_sum.11
  8.2 0.7 select_reduce_fusion
  8.8 0.7 fusion.25
  9.5 0.2 convolution_convert_fusion.4
  9.7 1.0 %convolution_convert_fusion.2 = bf16[12,3584]{1,0:T(8,128)(2,1)S(1)} fusion(bf16[12,8]{0,1:T(8,128)(2,1)S(1)} %convolution_convert_fusion.4, bf16[8,3584]{1,0:T(8,128)(2,1)} %param.8), kind=kOutput, calls=%fused_computation.4 | convolution fusion | flops 731136 | bytes 143552 | tf_op jit(solution)/shard_map/dot_general | solution.py:80
  10.8 0.7 broadcast_in_dim.28
  11.5 6.3 %all-to-all-start = ((bf16[4,6,3584]{2,1,0:T(8,128)(2,1)}), bf16[4,6,3584]{2,1,0:T(8,128)(2,1)S(1)}, u32[]{:S(2)}, u32[]{:S(2)}) async-start(bf16[4,6,3584]{2,1,0:T(8,128)(2,1)} %bitcast.5), calls=%async_computation | async-start | bytes 458752 | tf_op jit(solution)/shard_map/all_to_all | solution.py:94
  17.8 1.0 %convolution_convert_fusion.1 = bf16[12,3584]{1,0:T(8,128)(2,1)S(1)} fusion(bf16[12,8]{0,1:T(8,128)(2,1)S(1)} %convolution_convert_fusion.4, bf16[8,3584]{1,0:T(8,128)(2,1)} %param.9), kind=kOutput, calls=%fused_computation.3 | convolution fusion | flops 731136 | bytes 143552 | tf_op jit(solution)/shard_map/dot_general | solution.py:81
  18.9 7.1 %all-to-all-done = bf16[4,6,3584]{2,1,0:T(8,128)(2,1)S(1)} async-done(((bf16[4,6,3584]{2,1,0:T(8,128)(2,1)}), bf16[4,6,3584]{2,1,0:T(8,128)(2,1)S(1)}, u32[]{:S(2)}, u32[]{:S(2)}) %all-to-all-start) | async-done | bytes 172064 | tf_op jit(solution)/shard_map/all_to_all | solution.py:94
  26.0 0.7 broadcast_in_dim.29
  26.7 3.4 %all-to-all-start.2 = ((bf16[4,6,3584]{2,1,0:T(8,128)(2,1)}), bf16[4,6,3584]{2,1,0:T(8,128)(2,1)S(1)}, u32[]{:S(2)}, u32[]{:S(2)}) async-start(bf16[4,6,3584]{2,1,0:T(8,128)(2,1)} %bitcast.10), calls=%async_computation.3 | async-start | bytes 458752 | tf_op jit(solution)/shard_map/all_to_all | solution.py:95
  30.2 6.2 %all_gather.6 = bf16[48,3584]{1,0:T(8,128)(2,1)S(1)} all-gather(bf16[24,3584]{1,0:T(8,128)(2,1)S(1)} %all_to_all.30), channel_id=1, replica_groups=mesh['pipe'=4,'expert'=4,'dp'=2] {'dp'}, dimensions={0}, use_global_device_ids=true | all-gather | bytes 516096 | tf_op jit(solution)/shard_map/all_gather | solution.py:36
  36.4 0.4 fusion.13
  36.9 0.4 fusion.9
  37.4 6.1 %all_gather.7 = bf16[48,3584]{1,0:T(8,128)(2,1)S(1)} all-gather(bf16[24,3584]{1,0:T(8,128)(2,1)S(1)} %all_to_all.35), channel_id=1, replica_groups=mesh['pipe'=4,'expert'=4,'dp'=2] {'dp'}, dimensions={0}, use_global_device_ids=true | all-gather | bytes 516096 | tf_op jit(solution)/shard_map/all_gather | solution.py:37
  43.5 2.1 %fusion.5 = f32[48,256]{1,0:T(8,128)S(1)} fusion(bf16[48,3584]{1,0:T(8,128)(2,1)S(1)} %all_gather.7, bf16[1,1,256,3584]{3,2,1,0:T(8,128)(2,1)} %param.15), kind=kOutput, calls=%fused_computation.11 | convolution fusion | flops 88080384 | bytes 2228224 | tf_op jit(solution)/shard_map/dot_general | solution.py:19
  45.6 0.6 fusion.11
  46.3 0.9 copy-done.2
  47.1 1.4 %fusion = bf16[48,3584]{1,0:T(8,128)(2,1)} fusion(f32[48,3584]{1,0:T(8,128)S(1)} %fusion.11, bf16[1,1,3584,256]{3,2,1,0:T(8,128)(2,1)S(1)} %copy-done.2, f32[48,256]{1,0:T(8,128)S(1)} %fusion.5, f32[48,256]{1,0:T(8,128)S(1)} %fusion.13), kind=kOutput, calls=%fused_computation.1 | convolution fusion | flops 88498176 | bytes 2965504 | tf_op jit(solution)/shard_map/dot_general | solution.py:28
  48.6 2.6 %convolution_convert_fusion = bf16[48,3584]{1,0:T(8,128)(2,1)} fusion(bf16[1,1,256,3584]{3,2,1,0:T(8,128)(2,1)} %param.15, f32[48,256]{1,0:T(8,128)S(1)} %fusion.9, f32[48,256]{1,0:T(8,128)S(1)} %fusion.13), kind=kOutput, calls=%fused_computation.2 | convolution fusion | flops 88326144 | bytes 2277376 | tf_op jit(solution)/shard_map/dot_general | solution.py:24
  51.3 11.4 %reduce-scatter.5.cloned.1.call-done = bf16[24,3584]{1,0:T(8,128)(2,1)} async-done(((bf16[48,3584]{1,0:T(8,128)(2,1)}), bf16[24,3584]{1,0:T(8,128)(2,1)}) %reduce-scatter.5.cloned.1.call-update) | async-done | bytes 172048 | tf_op jit(solution)/shard_map/reduce_scatter | solution.py:44
  62.7 1.7 %all_to_all.36 = bf16[4,6,3584]{2,1,0:T(8,128)(2,1)} reshape(bf16[24,3584]{1,0:T(8,128)(2,1)} %reduce-scatter.5.cloned.1.call-done) | data formatting | bytes 344064 | tf_op jit(solution)/shard_map/all_to_all | solution.py:100
  64.3 4.6 %all-to-all-start.3 = ((bf16[4,6,3584]{2,1,0:T(8,128)(2,1)}), bf16[4,6,3584]{2,1,0:T(8,128)(2,1)S(1)}, u32[]{:S(2)}, u32[]{:S(2)}) async-start(bf16[4,6,3584]{2,1,0:T(8,128)(2,1)} %all_to_all.36), calls=%async_computation.5 | async-start | bytes 458752 | tf_op jit(solution)/shard_map/all_to_all | solution.py:100
  69.6 0.2 convolution_convert_fusion.3
  69.8 7.9 %reduce-scatter.3.cloned.1.call-done = bf16[24,3584]{1,0:T(8,128)(2,1)} async-done(((bf16[48,3584]{1,0:T(8,128)(2,1)}), bf16[24,3584]{1,0:T(8,128)(2,1)}) %reduce-scatter.3.cloned.1.call-update) | async-done | bytes 172048 | tf_op jit(solution)/shard_map/reduce_scatter | solution.py:41
  77.6 1.7 %all_to_all.31 = bf16[4,6,3584]{2,1,0:T(8,128)(2,1)} reshape(bf16[24,3584]{1,0:T(8,128)(2,1)} %reduce-scatter.3.cloned.1.call-done) | data formatting | bytes 344064 | tf_op jit(solution)/shard_map/all_to_all | solution.py:99
  79.3 4.6 %all-to-all-start.1 = ((bf16[4,6,3584]{2,1,0:T(8,128)(2,1)}), bf16[4,6,3584]{2,1,0:T(8,128)(2,1)S(1)}, u32[]{:S(2)}, u32[]{:S(2)}) async-start(bf16[4,6,3584]{2,1,0:T(8,128)(2,1)} %all_to_all.31), calls=%async_computation.2 | async-start | bytes 458752 | tf_op jit(solution)/shard_map/all_to_all | solution.py:99
  84.1 1.3 %collective-permute-start = (bf16[8,3584]{1,0:T(8,128)(2,1)S(1)}, bf16[8,3584]{1,0:T(8,128)(2,1)S(1)}, u32[]{:S(2)}, u32[]{:S(2)}) collective-permute-start(bf16[8,3584]{1,0:T(8,128)(2,1)S(1)} %fusion.4), channel_id=1, source_target_pairs={{8,0},{16,8},{24,16},{9,1},{17,9},{25,17},{10,2},{18,10},{26,18},{... | collective-permute-start | bytes 172040 | tf_op jit(solution)/shard_map/ppermute | solution.py:10
  85.4 6.7 %all-to-all-done.1 = bf16[4,6,3584]{2,1,0:T(8,128)(2,1)S(1)} async-done(((bf16[4,6,3584]{2,1,0:T(8,128)(2,1)}), bf16[4,6,3584]{2,1,0:T(8,128)(2,1)S(1)}, u32[]{:S(2)}, u32[]{:S(2)}) %all-to-all-start.1) | async-done | bytes 172064 | tf_op jit(solution)/shard_map/all_to_all | solution.py:99
  92.2 0.8 fusion.3
  93.0 0.6 copy.12
  (27 shorter events, 0.7 us)
Async XLA Ops:
  7.2 29.3 %copy-start = (bf16[1,1,3584,256]{3,2,1,0:T(8,128)(2,1)S(1)}, bf16[1,1,3584,256]{3,2,1,0:T(8,128)(2,1)}, u32[]{:S(2)}) copy-start(bf16[1,1,3584,256]{3,2,1,0:T(8,128)(2,1)} %param.13) | copy-start | bytes 5505028
  11.5 14.5 %all-to-all-start = ((bf16[4,6,3584]{2,1,0:T(8,128)(2,1)}), bf16[4,6,3584]{2,1,0:T(8,128)(2,1)S(1)}, u32[]{:S(2)}, u32[]{:S(2)}) async-start(bf16[4,6,3584]{2,1,0:T(8,128)(2,1)} %bitcast.5), calls=%async_computation | async-start | bytes 458752 | tf_op jit(solution)/shard_map/all_to_all | solution.py:94
  26.7 10.6 %all-to-all-start.2 = ((bf16[4,6,3584]{2,1,0:T(8,128)(2,1)}), bf16[4,6,3584]{2,1,0:T(8,128)(2,1)S(1)}, u32[]{:S(2)}, u32[]{:S(2)}) async-start(bf16[4,6,3584]{2,1,0:T(8,128)(2,1)} %bitcast.10), calls=%async_computation.3 | async-start | bytes 458752 | tf_op jit(solution)/shard_map/all_to_all | solution.py:95
  30.1 32.6 %reduce-scatter.5.cloned.1.call-start = ((), (), s32[]{:S(2)}) async-start(), calls=%async_computation.7 | async-start | bytes 516096 | tf_op jit(solution)/shard_map/reduce_scatter | solution.py:44
  30.2 6.7 %copy-start.1 = (bf16[1,1,3584,256]{3,2,1,0:T(8,128)(2,1)S(1)}, bf16[1,1,3584,256]{3,2,1,0:T(8,128)(2,1)}, u32[]{:S(2)}) copy-start(bf16[1,1,3584,256]{3,2,1,0:T(8,128)(2,1)} %param.14) | copy-start | bytes 5505028
  45.6 1.5 %copy-start.2 = (bf16[1,1,3584,256]{3,2,1,0:T(8,128)(2,1)S(1)}, bf16[1,1,3584,256]{3,2,1,0:T(8,128)(2,1)}, u32[]{:S(2)}) copy-start(bf16[1,1,3584,256]{3,2,1,0:T(8,128)(2,1)} %param.14) | copy-start | bytes 5505028
  48.5 21.1 %copy-start.5 = (bf16[8,1]{0,1:T(2,128)(2,1)S(1)}, bf16[8,1]{0,1:T(2,128)(2,1)}, u32[]{:S(2)}) copy-start(bf16[8,1]{0,1:T(2,128)(2,1)} %param.11) | copy-start | bytes 52
  48.6 29.1 %reduce-scatter.3.cloned.1.call-start = ((), (), s32[]{:S(2)}) async-start(), calls=%async_computation.6 | async-start | bytes 516096 | tf_op jit(solution)/shard_map/reduce_scatter | solution.py:41
  51.2 32.8 %copy-start.3 = (bf16[8,3584]{1,0:T(8,128)(2,1)S(1)}, bf16[8,3584]{1,0:T(8,128)(2,1)}, u32[]{:S(2)}) copy-start(bf16[8,3584]{1,0:T(8,128)(2,1)} %param.9) | copy-start | bytes 172036
  51.2 41.0 %copy-start.4 = (bf16[8,3584]{1,0:T(8,128)(2,1)S(1)}, bf16[8,3584]{1,0:T(8,128)(2,1)}, u32[]{:S(2)}) copy-start(bf16[8,3584]{1,0:T(8,128)(2,1)} %param.8) | copy-start | bytes 172036
  64.3 14.9 %all-to-all-start.3 = ((bf16[4,6,3584]{2,1,0:T(8,128)(2,1)}), bf16[4,6,3584]{2,1,0:T(8,128)(2,1)S(1)}, u32[]{:S(2)}, u32[]{:S(2)}) async-start(bf16[4,6,3584]{2,1,0:T(8,128)(2,1)} %all_to_all.36), calls=%async_computation.5 | async-start | bytes 458752 | tf_op jit(solution)/shard_map/all_to_all | solution.py:100
  79.3 12.8 %all-to-all-start.1 = ((bf16[4,6,3584]{2,1,0:T(8,128)(2,1)}), bf16[4,6,3584]{2,1,0:T(8,128)(2,1)S(1)}, u32[]{:S(2)}, u32[]{:S(2)}) async-start(bf16[4,6,3584]{2,1,0:T(8,128)(2,1)} %all_to_all.31), calls=%async_computation.2 | async-start | bytes 458752 | tf_op jit(solution)/shard_map/all_to_all | solution.py:99
  84.1 8.8 %collective-permute-start = (bf16[8,3584]{1,0:T(8,128)(2,1)S(1)}, bf16[8,3584]{1,0:T(8,128)(2,1)S(1)}, u32[]{:S(2)}, u32[]{:S(2)}) collective-permute-start(bf16[8,3584]{1,0:T(8,128)(2,1)S(1)} %fusion.4), channel_id=1, source_target_pairs={{8,0},{16,8},{24,16},{9,1},{17,9},{25,17},{10,2},{18,10},{26,18},{... | collective-permute-start | bytes 172040 | tf_op jit(solution)/shard_map/ppermute | solution.py:10
Sparse Core Ops, SparseCore 0:
  48.7 13.9 reduce-scatter.4
  64.9 12.6 reduce-scatter.2
where the time goes:
time: 101 us; the launch traced here: 100 us
  waiting for transfers between devices  33.1 us (33%)
  starting transfers between devices  20.3 us (20%)
  between operations  14.9 us (15%)
  blocking collectives  12.3 us (12%)
  matrix products  11 us (11%)
  local copies, waits for them, and re-layouts  6.49 us (6%)
  other arithmetic  2.4 us (2%)
    reduce_scatter x1, waiting for transfers between devices, shared_rows(): lax.psum_scatter(partial_gradient.astype(jnp.bfloat16), 'dp', scatter_dim...  11.4 us
    reduce_scatter x1, waiting for transfers between devices, shared_rows(): lax.psum_scatter(part_out.astype(jnp.bfloat16), 'dp', scatter_dimension=0...  7.88 us
    all_to_all x1, waiting for transfers between devices, shards(): lax.all_to_all(send_in, 'expert', split_axis=0, concat_axis=0, tiled=True)  7.13 us
    all_to_all x1, waiting for transfers between devices, shards(): lax.all_to_all(half_out, 'expert', split_axis=0, concat_axis=0, tiled=True)  6.68 us
    all_to_all x1, starting transfers between devices, shards(): lax.all_to_all(send_in, 'expert', split_axis=0, concat_axis=0, tiled=True)  6.32 us
    all_gather x1, blocking collectives, shared_rows(): lax.all_gather(input_rows, 'dp', axis=0, tiled=True)  6.22 us
    all_gather x1, blocking collectives, shared_rows(): lax.all_gather(rows_cot, 'dp', axis=0, tiled=True)  6.08 us
    all_to_all x1, starting transfers between devices, shards(): lax.all_to_all(half_out, 'expert', split_axis=0, concat_axis=0, tiled=True)  4.61 us
  transfers between devices with their start and end apart: 7, of which 4 were waited for; matrix products, arithmetic and copies ran while one was open for 6% of the time, Pallas kernels for 0%

commit v1 on v0

--- a/solution.py
+++ b/solution.py
@@ -90,9 +90,24 @@
     send_cot = jnp.repeat(packed_cot.reshape(experts, capacity, width), 2, axis=0).reshape(
         n_expert * capacity, width
     )
+
+    def core_do(body):
+        z_new, x_new = (lax.axis_size("expert"), lax.axis_index("expert"))
+        f_next = body.shape[0] // z_new
+        new = jnp.roll(body, -x_new * f_next, axis=0)
+        all_rows = [lax.slice_in_dim(new, 0, f_next, axis=0)]
+        for nth in range(1, z_new):
+            met_up = lax.slice_in_dim(new, nth * f_next, (nth + 1) * f_next, axis=0)
+            all_rows.append(
+                lax.ppermute(met_up, "expert", [(b, (b + nth) % z_new) for b in range(z_new)])
+            )
+        return jnp.roll(
+            jnp.concatenate(all_rows[::-1], axis=0), (x_new + 1) * all_rows[0].shape[0], axis=0
+        )
+
     got_in, got_cot = (
         lax.all_to_all(send_in, "expert", split_axis=0, concat_axis=0, tiled=True),
-        lax.all_to_all(send_cot, "expert", split_axis=0, concat_axis=0, tiled=True),
+        core_do(send_cot),
     )
     half_out, half_grad = shared_rows(got_in, got_cot, gate_cols, up_cols, down_rows)
     back_out, back_grad = (

time: 101 us -> 93 us (0.921)
  waiting for transfers between devices: 33.1 us -> 25.9 us
  local copies, waits for them, and re-layouts: 6.49 us -> 4.99 us
    all_to_all x1, waiting for transfers between devices: 7.13 us -> 0.01 us  [shards(): lax.all_to_all(send_in, 'expert', split_axis=0, concat_axis=0, tiled=True)]
    ppermute x0 -> x3, starting transfers between devices: none -> 6.11 us  [core_do(): lax.ppermute(met_up, 'expert', [(b, (b + nth) % z_new) for b in range(z_n...]
    all_to_all x1 -> x0, starting transfers between devices: 3.38 us -> none  [shards(): lax.all_to_all(send_cot, 'expert', split_axis=0, concat_axis=0, tiled=True)]
    all_to_all x1, starting transfers between devices: 6.32 us -> 4.08 us  [shards(): lax.all_to_all(send_in, 'expert', split_axis=0, concat_axis=0, tiled=True)]
  transfers between devices with their start and end apart: 7 -> 9, of which waited for: 4 -> 3; matrix products, arithmetic and copies ran while one was open for 6% -> 8% of each run, Pallas kernels for 0% -> 0%
where the time goes in v1:
time: 93 us; the launch traced here: 92.4 us
  waiting for transfers between devices  25.9 us (28%)
  starting transfers between devices  20.7 us (22%)
  between operations  14.9 us (16%)
  blocking collectives  12.3 us (13%)
  matrix products  10.2 us (11%)
  local copies, waits for them, and re-layouts  4.99 us (5%)
  other arithmetic  3.31 us (4%)
    reduce_scatter x1, waiting for transfers between devices, shared_rows(): lax.psum_scatter(partial_gradient.astype(jnp.bfloat16), 'dp', scatter_dim...  11.5 us
    reduce_scatter x1, waiting for transfers between devices, shared_rows(): lax.psum_scatter(part_out.astype(jnp.bfloat16), 'dp', scatter_dimension=0...  7.77 us
    all_to_all x1, waiting for transfers between devices, shards(): lax.all_to_all(half_out, 'expert', split_axis=0, concat_axis=0, tiled=True)  6.67 us
    all_gather x1, blocking collectives, shared_rows(): lax.all_gather(input_rows, 'dp', axis=0, tiled=True)  6.22 us
    ppermute x3, starting transfers between devices, core_do(): lax.ppermute(met_up, 'expert', [(b, (b + nth) % z_new) for b in range(z_n...  6.11 us
    all_gather x1, blocking collectives, shared_rows(): lax.all_gather(rows_cot, 'dp', axis=0, tiled=True)  6.08 us
    all_to_all x1, starting transfers between devices, shards(): lax.all_to_all(half_grad, 'expert', split_axis=0, concat_axis=0, tiled=True)  4.61 us
    all_to_all x1, starting transfers between devices, shards(): lax.all_to_all(half_out, 'expert', split_axis=0, concat_axis=0, tiled=True)  4.61 us
  transfers between devices with their start and end apart: 9, of which 3 were waited for; matrix products, arithmetic and copies ran while one was open for 8% of the time, Pallas kernels for 0%

profile of v1, /device:TPU:0, one launch (start us, length us, event | category | flops | bytes accessed | tf_op | source)
XLA Modules:
  0.0 92.4 jit_solution(9195618538789516800)
XLA Ops:
  7.2 0.8 fusion.32
  8.0 0.2 reduce_window_sum.11
  8.2 0.7 select_reduce_fusion
  8.9 0.7 fusion.33
  9.5 0.2 convolution_convert_fusion.4
  9.7 1.0 %convolution_convert_fusion.1 = bf16[12,3584]{1,0:T(8,128)(2,1)S(1)} fusion(bf16[12,8]{0,1:T(8,128)(2,1)S(1)} %convolution_convert_fusion.4, bf16[8,3584]{1,0:T(8,128)(2,1)} %param.11), kind=kOutput, calls=%fused_computation.3 | convolution fusion | flops 731136 | bytes 143552 | tf_op jit(solution)/shard_map/dot_general | solution.py:81
  11.1 5.1 %collective-permute-start = (bf16[6,3584]{1,0:T(8,128)(2,1)S(1)}, bf16[6,3584]{1,0:T(8,128)(2,1)S(1)}, u32[]{:S(2)}, u32[]{:S(2)}) collective-permute-start(bf16[6,3584]{1,0:T(8,128)(2,1)S(1)} %get-tuple-element.6), channel_id=1, source_target_pairs={{0,6},{2,0},{4,2},{6,4},{1,7},{3,1},{5,3},{7,5},{8,14},{10,8},{12,... | collective-permute-start | bytes 129032 | tf_op jit(solution)/shard_map/ppermute | solution.py:102
  16.2 1.0 %collective-permute-start.2 = (bf16[6,3584]{1,0:T(8,128)(2,1)S(1)}, bf16[6,3584]{1,0:T(8,128)(2,1)S(1)}, u32[]{:S(2)}, u32[]{:S(2)}) collective-permute-start(bf16[6,3584]{1,0:T(8,128)(2,1)S(1)} %get-tuple-element.4), channel_id=1, source_target_pairs={{0,2},{2,4},{4,6},{6,0},{1,3},{3,5},{5,7},{7,1},{8,10},{10,12},{12... | collective-permute-start | bytes 129032 | tf_op jit(solution)/shard_map/ppermute | solution.py:102
  17.2 0.2 convolution_convert_fusion.2
  17.5 0.7 broadcast_in_dim.28
  18.2 4.1 %all-to-all-start = ((bf16[4,6,3584]{2,1,0:T(8,128)(2,1)}), bf16[4,6,3584]{2,1,0:T(8,128)(2,1)S(1)}, u32[]{:S(2)}, u32[]{:S(2)}) async-start(bf16[4,6,3584]{2,1,0:T(8,128)(2,1)} %bitcast.5), calls=%async_computation | async-start | bytes 458752 | tf_op jit(solution)/shard_map/all_to_all | solution.py:109
  22.3 0.8 fusion.18
  23.1 6.1 %all_gather.7 = bf16[48,3584]{1,0:T(8,128)(2,1)S(1)} all-gather(bf16[24,3584]{1,0:T(8,128)(2,1)S(1)} %fusion.18), channel_id=1, replica_groups=mesh['pipe'=4,'expert'=4,'dp'=2] {'dp'}, dimensions={0}, use_global_device_ids=true | all-gather | bytes 516096 | tf_op jit(solution)/shard_map/all_gather | solution.py:37
  29.2 2.1 %fusion.5 = f32[48,256]{1,0:T(8,128)S(1)} fusion(bf16[48,3584]{1,0:T(8,128)(2,1)S(1)} %all_gather.7, bf16[1,1,256,3584]{3,2,1,0:T(8,128)(2,1)} %param.17), kind=kOutput, calls=%fused_computation.11 | convolution fusion | flops 88080384 | bytes 2228224 | tf_op jit(solution)/shard_map/dot_general | solution.py:19
  31.4 6.2 %all_gather.6 = bf16[48,3584]{1,0:T(8,128)(2,1)S(1)} all-gather(bf16[24,3584]{1,0:T(8,128)(2,1)S(1)} %all_to_all.22), channel_id=1, replica_groups=mesh['pipe'=4,'expert'=4,'dp'=2] {'dp'}, dimensions={0}, use_global_device_ids=true | all-gather | bytes 516096 | tf_op jit(solution)/shard_map/all_gather | solution.py:36
  37.6 0.4 fusion.13
  38.1 0.4 fusion.9
  38.5 0.6 fusion.11
  39.1 1.4 %fusion = bf16[48,3584]{1,0:T(8,128)(2,1)} fusion(f32[48,3584]{1,0:T(8,128)S(1)} %fusion.11, bf16[1,1,3584,256]{3,2,1,0:T(8,128)(2,1)S(1)} %copy-done.1, f32[48,256]{1,0:T(8,128)S(1)} %fusion.5, f32[48,256]{1,0:T(8,128)S(1)} %fusion.13), kind=kOutput, calls=%fused_computation.1 | convolution fusion | flops 88498176 | bytes 2965504 | tf_op jit(solution)/shard_map/dot_general | solution.py:28
  40.6 2.6 %convolution_convert_fusion = bf16[48,3584]{1,0:T(8,128)(2,1)} fusion(bf16[1,1,256,3584]{3,2,1,0:T(8,128)(2,1)} %param.17, f32[48,256]{1,0:T(8,128)S(1)} %fusion.9, f32[48,256]{1,0:T(8,128)S(1)} %fusion.13), kind=kOutput, calls=%fused_computation.2 | convolution fusion | flops 88326144 | bytes 2277376 | tf_op jit(solution)/shard_map/dot_general | solution.py:24
  43.3 11.5 %reduce-scatter.5.cloned.1.call-done = bf16[24,3584]{1,0:T(8,128)(2,1)} async-done(((bf16[48,3584]{1,0:T(8,128)(2,1)}), bf16[24,3584]{1,0:T(8,128)(2,1)}) %reduce-scatter.5.cloned.1.call-update) | async-done | bytes 172048 | tf_op jit(solution)/shard_map/reduce_scatter | solution.py:44
  54.7 1.7 %all_to_all.25 = bf16[4,6,3584]{2,1,0:T(8,128)(2,1)} reshape(bf16[24,3584]{1,0:T(8,128)(2,1)} %reduce-scatter.5.cloned.1.call-done) | data formatting | bytes 344064 | tf_op jit(solution)/shard_map/all_to_all | solution.py:115
  56.4 4.6 %all-to-all-start.2 = ((bf16[4,6,3584]{2,1,0:T(8,128)(2,1)}), bf16[4,6,3584]{2,1,0:T(8,128)(2,1)S(1)}, u32[]{:S(2)}, u32[]{:S(2)}) async-start(bf16[4,6,3584]{2,1,0:T(8,128)(2,1)} %all_to_all.25), calls=%async_computation.4 | async-start | bytes 458752 | tf_op jit(solution)/shard_map/all_to_all | solution.py:115
  61.7 0.2 convolution_convert_fusion.3
  61.8 7.8 %reduce-scatter.3.cloned.1.call-done = bf16[24,3584]{1,0:T(8,128)(2,1)} async-done(((bf16[48,3584]{1,0:T(8,128)(2,1)}), bf16[24,3584]{1,0:T(8,128)(2,1)}) %reduce-scatter.3.cloned.1.call-update) | async-done | bytes 172048 | tf_op jit(solution)/shard_map/reduce_scatter | solution.py:41
  69.6 1.7 %all_to_all.23 = bf16[4,6,3584]{2,1,0:T(8,128)(2,1)} reshape(bf16[24,3584]{1,0:T(8,128)(2,1)} %reduce-scatter.3.cloned.1.call-done) | data formatting | bytes 344064 | tf_op jit(solution)/shard_map/all_to_all | solution.py:114
  71.3 4.6 %all-to-all-start.1 = ((bf16[4,6,3584]{2,1,0:T(8,128)(2,1)}), bf16[4,6,3584]{2,1,0:T(8,128)(2,1)S(1)}, u32[]{:S(2)}, u32[]{:S(2)}) async-start(bf16[4,6,3584]{2,1,0:T(8,128)(2,1)} %all_to_all.23), calls=%async_computation.2 | async-start | bytes 458752 | tf_op jit(solution)/shard_map/all_to_all | solution.py:114
  76.0 0.1 fusion.4
  76.1 1.3 %collective-permute-start.3 = (bf16[8,3584]{1,0:T(8,128)(2,1)S(1)}, bf16[8,3584]{1,0:T(8,128)(2,1)S(1)}, u32[]{:S(2)}, u32[]{:S(2)}) collective-permute-start(bf16[8,3584]{1,0:T(8,128)(2,1)S(1)} %fusion.4), channel_id=1, source_target_pairs={{8,0},{16,8},{24,16},{9,1},{17,9},{25,17},{10,2},{18,10},{26,18},{... | collective-permute-start | bytes 172040 | tf_op jit(solution)/shard_map/ppermute | solution.py:10
  77.4 6.7 %all-to-all-done.1 = bf16[4,6,3584]{2,1,0:T(8,128)(2,1)S(1)} async-done(((bf16[4,6,3584]{2,1,0:T(8,128)(2,1)}), bf16[4,6,3584]{2,1,0:T(8,128)(2,1)S(1)}, u32[]{:S(2)}, u32[]{:S(2)}) %all-to-all-start.1) | async-done | bytes 172064 | tf_op jit(solution)/shard_map/all_to_all | solution.py:114
  84.2 0.8 fusion.3
  85.0 0.6 copy.12
  (32 shorter events, 0.7 us)
Async XLA Ops:
  7.2 30.4 %copy-start = (bf16[1,1,3584,256]{3,2,1,0:T(8,128)(2,1)S(1)}, bf16[1,1,3584,256]{3,2,1,0:T(8,128)(2,1)}, u32[]{:S(2)}) copy-start(bf16[1,1,3584,256]{3,2,1,0:T(8,128)(2,1)} %param.15) | copy-start | bytes 5505028
  7.2 10.0 %copy-start.3 = (bf16[8,3584]{1,0:T(8,128)(2,1)S(1)}, bf16[8,3584]{1,0:T(8,128)(2,1)}, u32[]{:S(2)}) copy-start(bf16[8,3584]{1,0:T(8,128)(2,1)} %param.10) | copy-start | bytes 172036
  11.1 11.2 %collective-permute-start = (bf16[6,3584]{1,0:T(8,128)(2,1)S(1)}, bf16[6,3584]{1,0:T(8,128)(2,1)S(1)}, u32[]{:S(2)}, u32[]{:S(2)}) collective-permute-start(bf16[6,3584]{1,0:T(8,128)(2,1)S(1)} %get-tuple-element.6), channel_id=1, source_target_pairs={{0,6},{2,0},{4,2},{6,4},{1,7},{3,1},{5,3},{7,5},{8,14},{10,8},{12,... | collective-permute-start | bytes 129032 | tf_op jit(solution)/shard_map/ppermute | solution.py:102
  16.2 6.1 %collective-permute-start.1 = (bf16[6,3584]{1,0:T(8,128)(2,1)S(1)}, bf16[6,3584]{1,0:T(8,128)(2,1)S(1)}, u32[]{:S(2)}, u32[]{:S(2)}) collective-permute-start(bf16[6,3584]{1,0:T(8,128)(2,1)S(1)} %get-tuple-element.5), channel_id=1, source_target_pairs={{0,4},{2,6},{4,0},{6,2},{1,5},{3,7},{5,1},{7,3},{8,12},{10,14},{12... | collective-permute-start | bytes 129032 | tf_op jit(solution)/shard_map/ppermute | solution.py:102
  16.2 6.1 %collective-permute-start.2 = (bf16[6,3584]{1,0:T(8,128)(2,1)S(1)}, bf16[6,3584]{1,0:T(8,128)(2,1)S(1)}, u32[]{:S(2)}, u32[]{:S(2)}) collective-permute-start(bf16[6,3584]{1,0:T(8,128)(2,1)S(1)} %get-tuple-element.4), channel_id=1, source_target_pairs={{0,2},{2,4},{4,6},{6,0},{1,3},{3,5},{5,7},{7,1},{8,10},{10,12},{12... | collective-permute-start | bytes 129032 | tf_op jit(solution)/shard_map/ppermute | solution.py:102
  18.2 13.1 %all-to-all-start = ((bf16[4,6,3584]{2,1,0:T(8,128)(2,1)}), bf16[4,6,3584]{2,1,0:T(8,128)(2,1)S(1)}, u32[]{:S(2)}, u32[]{:S(2)}) async-start(bf16[4,6,3584]{2,1,0:T(8,128)(2,1)} %bitcast.5), calls=%async_computation | async-start | bytes 458752 | tf_op jit(solution)/shard_map/all_to_all | solution.py:109
  22.3 32.5 %reduce-scatter.5.cloned.1.call-start = ((), (), s32[]{:S(2)}) async-start(), calls=%async_computation.6 | async-start | bytes 516096 | tf_op jit(solution)/shard_map/reduce_scatter | solution.py:44
  31.4 6.7 %copy-start.1 = (bf16[1,1,3584,256]{3,2,1,0:T(8,128)(2,1)S(1)}, bf16[1,1,3584,256]{3,2,1,0:T(8,128)(2,1)}, u32[]{:S(2)}) copy-start(bf16[1,1,3584,256]{3,2,1,0:T(8,128)(2,1)} %param.16) | copy-start | bytes 5505028
  40.5 21.1 %copy-start.4 = (bf16[8,1]{0,1:T(2,128)(2,1)S(1)}, bf16[8,1]{0,1:T(2,128)(2,1)}, u32[]{:S(2)}) copy-start(bf16[8,1]{0,1:T(2,128)(2,1)} %param.13) | copy-start | bytes 52
  40.6 29.0 %reduce-scatter.3.cloned.1.call-start = ((), (), s32[]{:S(2)}) async-start(), calls=%async_computation.5 | async-start | bytes 516096 | tf_op jit(solution)/shard_map/reduce_scatter | solution.py:41
  43.3 32.7 %copy-start.2 = (bf16[8,3584]{1,0:T(8,128)(2,1)S(1)}, bf16[8,3584]{1,0:T(8,128)(2,1)}, u32[]{:S(2)}) copy-start(bf16[8,3584]{1,0:T(8,128)(2,1)} %param.11) | copy-start | bytes 172036
  56.4 14.9 %all-to-all-start.2 = ((bf16[4,6,3584]{2,1,0:T(8,128)(2,1)}), bf16[4,6,3584]{2,1,0:T(8,128)(2,1)S(1)}, u32[]{:S(2)}, u32[]{:S(2)}) async-start(bf16[4,6,3584]{2,1,0:T(8,128)(2,1)} %all_to_all.25), calls=%async_computation.4 | async-start | bytes 458752 | tf_op jit(solution)/shard_map/all_to_all | solution.py:115
  71.3 12.8 %all-to-all-start.1 = ((bf16[4,6,3584]{2,1,0:T(8,128)(2,1)}), bf16[4,6,3584]{2,1,0:T(8,128)(2,1)S(1)}, u32[]{:S(2)}, u32[]{:S(2)}) async-start(bf16[4,6,3584]{2,1,0:T(8,128)(2,1)} %all_to_all.23), calls=%async_computation.2 | async-start | bytes 458752 | tf_op jit(solution)/shard_map/all_to_all | solution.py:114
  76.1 8.8 %collective-permute-start.3 = (bf16[8,3584]{1,0:T(8,128)(2,1)S(1)}, bf16[8,3584]{1,0:T(8,128)(2,1)S(1)}, u32[]{:S(2)}, u32[]{:S(2)}) collective-permute-start(bf16[8,3584]{1,0:T(8,128)(2,1)S(1)} %fusion.4), channel_id=1, source_target_pairs={{8,0},{16,8},{24,16},{9,1},{17,9},{25,17},{10,2},{18,10},{26,18},{... | collective-permute-start | bytes 172040 | tf_op jit(solution)/shard_map/ppermute | solution.py:10
Sparse Core Ops, SparseCore 0:
  40.7 14.0 reduce-scatter.4
  57.0 12.5 reduce-scatter.2
